TPU v7x, 32 devices: a whole 2x2x4 slice. The times are simulated.
32 devices in a mesh: grp: 4 (over y, core), dev: 8 (over z, x).
Axes of the slice: x: 2, y: 2, z: 4, core: 2. Of those that a mesh axis runs over, the one named last changes fastest.
Arguments:
- centers: bfloat16 [4096, 128], P(('grp', 'dev')), may hold values from -4 to 4
- center_weights: bfloat16 [4096, 64], P(('grp', 'dev')), may hold values from -0.75 to 0.75
- batch: bfloat16 [8192, 128], P('dev'), may hold values from -4 to 4
- labels: bfloat16 [8192, 64], P('dev'), may hold values from -6 to 6
- sub_centers: bfloat16 [2048, 128], P('grp'), may hold values from -4 to 4
- eig_vectors: bfloat16 [2048, 160], P('grp'), may hold values from -0.5 to 0.5
- eig_scale: float32 [160], replicated, may hold values from 0.02 to 0.4
Outputs:
- predictions: float32 [8192, 64], P('dev')
- center_step: float32 [4096, 64], P(('grp', 'dev'))
- nystrom_fix: float32 [2048, 64], P('grp')
All inputs are finite; a program needn't handle non-finite values.
Results may differ from a plain program's by a relative error of at most 0.0031.
Values may be sent and summed in bfloat16 or wider, within the bound.
A program may use at most 64 MiB of HBM per device.

v0:
```python
import math
import jax
import jax.numpy as jnp
from jax import lax
from jax.sharding import PartitionSpec as P

gamma_scale = 0.25
learn_rate = 8.0


def sq_norms(points):
    return jnp.sum(jnp.square(points.astype(jnp.float32)), axis=1)


def kernel_tile(left, left_sq, right, right_sq):
    cross = lax.dot_general(
        left, right, (((1,), (1,)), ((), ())), preferred_element_type=jnp.float32
    )
    dist = left_sq[:, None] + right_sq[None, :] - 2.0 * cross
    return jnp.exp(-gamma_scale * dist).astype(jnp.bfloat16)


def body(centers, center_weights, batch, labels, sub_centers, eig_vectors, eig_scale):
    samples = batch.shape[0]
    width_in = batch.shape[1]
    width_out = labels.shape[1]
    block = min(512, samples)
    num_blocks = samples // block
    factor = learn_rate / math.sqrt(samples * lax.axis_size("dev"))
    batch_sq = sq_norms(batch)
    batch_blocks = batch.reshape(num_blocks, block, width_in)
    sq_blocks = batch_sq.reshape(num_blocks, block)
    group_centers, group_weights = (
        lax.all_gather(centers, "dev", axis=0, tiled=True),
        lax.all_gather(center_weights, "dev", axis=0, tiled=True),
    )
    group_sq = sq_norms(group_centers)

    def pred_rows(inputs):
        rows_x, rows_sq = inputs
        tile = kernel_tile(rows_x, rows_sq, group_centers, group_sq)
        return jnp.dot(tile, group_weights, preferred_element_type=jnp.float32)

    partial_pred = lax.map(pred_rows, (batch_blocks, sq_blocks)).reshape(samples, width_out)
    predictions = lax.psum(partial_pred, "grp")
    resid = (predictions - labels.astype(jnp.float32)).astype(jnp.bfloat16)
    resid_blocks = resid.reshape(num_blocks, block, width_out)
    rows_sq = group_sq

    def add_block(accum, inputs):
        rows_x, part_sq, rows_r = inputs
        tile = kernel_tile(group_centers, rows_sq, rows_x, part_sq)
        return (accum + jnp.dot(tile, rows_r, preferred_element_type=jnp.float32), None)

    result, _ = lax.scan(
        add_block,
        jnp.zeros((lax.axis_size("dev") * centers.shape[0], width_out), jnp.float32),
        (batch_blocks, sq_blocks, resid_blocks),
    )
    center_step = lax.psum_scatter(result, "dev", scatter_dimension=0, tiled=True) * factor
    sub_sq = sq_norms(sub_centers)

    def sub_block(accum, inputs):
        rows_x, rows_sq, rows_r = inputs
        tile = kernel_tile(sub_centers, sub_sq, rows_x, rows_sq)
        return (accum + jnp.dot(tile, rows_r, preferred_element_type=jnp.float32), None)

    sub_part, _ = lax.scan(
        sub_block,
        jnp.zeros((sub_centers.shape[0], width_out), jnp.float32),
        (batch_blocks, sq_blocks, resid_blocks),
    )
    sub_part = sub_part * factor
    vectors = eig_vectors.astype(jnp.float32)
    dims = (((0,), (0,)), ((), ()))
    proj_part = lax.dot_general(vectors, sub_part, dims, precision=lax.Precision.HIGHEST)
    proj = lax.psum(proj_part, ("grp", "dev"))
    nystrom_fix = jnp.dot(vectors, eig_scale[:, None] * proj, precision=lax.Precision.HIGHEST)
    return (predictions, center_step, nystrom_fix)


def solution(mesh):
    placed = (
        P(("grp", "dev"), None),
        P(("grp", "dev"), None),
        P("dev", None),
        P("dev", None),
        P("grp", None),
        P("grp", None),
        P(),
    )
    return jax.shard_map(
        body,
        mesh=mesh,
        in_specs=placed,
        out_specs=(P("dev", None), P(("grp", "dev"), None), P("grp", None)),
        check_vma=False,
    )
```

profile of v0, /device:TPU:0, one launch (start us, length us, event | category | flops | bytes accessed | tf_op | source)
XLA Modules:
  0.0 186.0 jit_solution(1019431074230919624)
XLA Ops:
  7.2 0.0 copy-start
  7.2 0.0 all-reduce.2.cloned.1.call-start
  7.2 0.0 copy-start.2
  7.2 32.9 %all_gather.6 = bf16[1024,128]{1,0:T(8,128)(2,1)S(1)} all-gather(bf16[128,128]{1,0:T(8,128)(2,1)} %param.13), channel_id=1, replica_groups=mesh['grp'=4,'dev'=8] {'dev'}, dimensions={0}, use_global_device_ids=true | all-gather | bytes 294912 | tf_op jit(solution)/shard_map/all_gather | solution.py:34
  40.1 0.0 copy-start.6
  40.1 0.2 multiply_reduce_fusion
  40.4 0.0 copy-done.2
  40.4 0.2 multiply_reduce_fusion.1
  40.6 0.3 copy-done.6
  40.9 0.1 copy.10
  41.0 30.7 %all_gather.7 = bf16[1024,64]{1,0:T(8,128)(2,1)S(1)} all-gather(bf16[128,64]{1,0:T(8,128)(2,1)S(1)} %copy.10), channel_id=1, replica_groups=mesh['grp'=4,'dev'=8] {'dev'}, dimensions={0}, use_global_device_ids=true | all-gather | bytes 147456 | tf_op jit(solution)/shard_map/all_gather | solution.py:35
  71.7 4.5 %while.32 = (s32[]{:T(128)}, f32[2,512,64]{1,0,2:T(2,128)S(1)}, f32[2,512]{1,0:T(2,128)S(1)}, f32[1024]{0:T(1024)S(1)}, bf16[2,512,128]{2,1,0:T(8,128)(2,1)S(1)}...) while((s32[]{:T(128)}, f32[2,512,64]{1,0,2:T(2,128)S(1)}, ...), condition=%wide.region_3.4_spmd, body=%wide.region_2.3_spmd.sunk | while | flops 203948032 | bytes 1321065 | solution.py:44
  71.7 0.9 fusion.81
  72.6 0.1 copy.22
  72.7 1.2 dynamic_update_slice.5
  74.0 0.9 fusion.81
  74.9 0.1 copy.22
  75.0 1.2 dynamic_update_slice.5
  76.2 0.8 copy.20
  77.0 0.0 copy-start.4
  77.0 0.0 copy-start.5
  77.0 0.0 all-reduce.2.cloned.1.call-update
  77.0 0.0 reduce-scatter.2.cloned.1.call-start
  77.1 0.8 copy-done.4
  77.9 0.1 multiply_reduce_fusion.2
  78.0 32.6 %all-reduce.2.cloned.1.call-done = f32[1024,64]{0,1:T(8,128)} async-done(((f32[1024,64]{0,1:T(8,128)}), f32[1024,64]{0,1:T(8,128)}) %all-reduce.2.cloned.1.call-update) | async-done | bytes 262160 | tf_op jit(solution)/shard_map/psum | solution.py:45
  110.6 0.0 copy-done.5
  110.6 1.0 subtract_convert_fusion
  111.6 0.2 copy.14
  111.8 1.8 while.33
  111.8 0.9 fusion.85
  112.7 0.9 fusion.85
  113.6 0.0 copy-start.3
  113.6 0.7 copy-done.3
  114.3 0.0 reduce-scatter.2.cloned.1.call-update
  114.3 1.3 while.34
  114.3 0.6 fusion.89
  115.0 0.6 fusion.89
  115.6 0.0 copy-done
  115.6 0.0 copy-start.7
  115.6 0.3 convolution_bitcast_fusion.1
  115.9 40.1 %psum.15 = f32[160,64]{1,0:T(8,128)S(1)} all-reduce(f32[160,64]{1,0:T(8,128)S(1)} %convolution_bitcast_fusion.1), channel_id=1, replica_groups=mesh['grp'=4,'dev'=8] {'grp','dev'}, use_global_device_ids=true, to_apply=%region_11.12 | all-reduce | flops 10240 | bytes 81920 | tf_op jit(solution)/shard_map/psum | solution.py:77
  156.0 0.0 copy-done.7
  156.0 0.0 copy-start.1
  156.0 1.0 convolution_bitcast_fusion
  157.0 20.0 %reduce-scatter.2.cloned.1.call-done = f32[128,64]{0,1:T(8,128)} async-done(((f32[1024,64]{0,1:T(8,128)}), f32[128,64]{0,1:T(8,128)}) %reduce-scatter.2.cloned.1.call-update) | async-done | bytes 32784 | tf_op jit(solution)/shard_map/reduce_scatter | solution.py:60
  177.0 1.4 broadcast_multiply_fusion
  178.4 0.0 copy-done.1
  178.4 0.7 copy.43
  (10 shorter events, 0.1 us)
Async XLA Ops:
  7.2 108.4 %copy-start = (bf16[512,160]{0,1:T(8,128)(2,1)S(1)}, bf16[512,160]{0,1:T(8,128)(2,1)}, u32[]{:S(2)}) copy-start(bf16[512,160]{0,1:T(8,128)(2,1)} %param.18) | copy-start | bytes 491524
  7.2 103.4 %all-reduce.2.cloned.1.call-start = ((), (), s32[]{:S(2)}) async-start(), calls=%async_computation.1 | async-start | bytes 524288 | tf_op jit(solution)/shard_map/psum | solution.py:45
  7.2 33.1 %copy-start.2 = (bf16[1024,128]{1,0:T(8,128)(2,1)S(1)}, bf16[1024,128]{1,0:T(8,128)(2,1)}, u32[]{:S(2)}) copy-start(bf16[1024,128]{1,0:T(8,128)(2,1)} %param.15) | copy-start | bytes 786436
  40.1 0.7 copy-start.6
  77.0 0.9 copy-start.4
  77.0 33.6 %copy-start.5 = (bf16[1024,64]{0,1:T(8,128)(2,1)S(1)}, bf16[1024,64]{0,1:T(8,128)(2,1)}, u32[]{:S(2)}) copy-start(bf16[1024,64]{0,1:T(8,128)(2,1)} %param.16) | copy-start | bytes 393220
  77.0 100.0 %reduce-scatter.2.cloned.1.call-start = ((), (), s32[]{:S(2)}) async-start(), calls=%async_computation.2 | async-start | bytes 294912 | tf_op jit(solution)/shard_map/reduce_scatter | solution.py:60
  113.6 0.7 copy-start.3
  115.6 40.4 %copy-start.7 = (f32[160]{0:T(256)S(1)}, f32[160]{0:T(256)}, u32[]{:S(2)}) copy-start(f32[160]{0:T(256)} %param.19) | copy-start | bytes 1924
  156.0 22.4 %copy-start.1 = (f32[1024,64]{0,1:T(8,128)S(1)}, f32[1024,64]{0,1:T(8,128)}, u32[]{:S(2)}) copy-start(f32[1024,64]{0,1:T(8,128)} %all-reduce.2.cloned.1.call-done) | copy-start | bytes 786436
Sparse Core Ops, SparseCore 0:
  77.1 33.4 all-reduce.1
  114.5 62.5 reduce-scatter.1
where the time goes:
time: 186 us
  blocking collectives  104 us (56%)
  waiting for transfers between devices  52.6 us (28%)
  between operations  14.2 us (8%)
  local copies, waits for them, and re-layouts  6.28 us (3%)
  matrix products  5.97 us (3%)
  other arithmetic  2.92 us (2%)
    psum x1, blocking collectives, body(): proj = lax.psum(proj_part, ('grp', 'dev'))  40.1 us
    all_gather x1, blocking collectives, body(): lax.all_gather(centers, 'dev', axis=0, tiled=True)  32.9 us
    psum x1, waiting for transfers between devices, body(): predictions = lax.psum(partial_pred, 'grp')  32.6 us
    all_gather x1, blocking collectives, body(): lax.all_gather(center_weights, 'dev', axis=0, tiled=True)  30.7 us
    reduce_scatter x1, waiting for transfers between devices, body(): lax.psum_scatter(result, 'dev', scatter_dimension=0, tiled=True) * factor  20 us
  transfers between devices with their start and end apart: 2, of which 2 were waited for; matrix products, arithmetic and copies ran while one was open for 1% of the time, Pallas kernels for 0%

commit v1 on v0

--- a/solution.py
+++ b/solution.py
@@ -42,7 +42,7 @@
         return jnp.dot(tile, group_weights, preferred_element_type=jnp.float32)
 
     partial_pred = lax.map(pred_rows, (batch_blocks, sq_blocks)).reshape(samples, width_out)
-    predictions = lax.psum(partial_pred, "grp")
+    predictions = jnp.sum(lax.all_gather(partial_pred, "grp"), axis=0)
     resid = (predictions - labels.astype(jnp.float32)).astype(jnp.bfloat16)
     resid_blocks = resid.reshape(num_blocks, block, width_out)
     rows_sq = group_sq

time: 186 us -> 172 us (0.925)
  waiting for transfers between devices: 52.6 us -> 37.8 us
    psum x1 -> x0, waiting for transfers between devices: 32.6 us -> none  [body(): predictions = lax.psum(partial_pred, 'grp')]
    all_gather x0 -> x1, waiting for transfers between devices: none -> 17.6 us  [body(): predictions = jnp.sum(lax.all_gather(partial_pred, 'grp'), axis=0)]
where the time goes in v1:
time: 172 us; the launch traced here: 171 us
  blocking collectives  103 us (60%)
  waiting for transfers between devices  37.8 us (22%)
  between operations  14.2 us (8%)
  local copies, waits for them, and re-layouts  5.86 us (3%)
  matrix products  5.65 us (3%)
  other arithmetic  4.24 us (2%)
    psum x1, blocking collectives, body(): proj = lax.psum(proj_part, ('grp', 'dev'))  39.6 us
    all_gather x1, blocking collectives, body(): lax.all_gather(centers, 'dev', axis=0, tiled=True)  32.9 us
    all_gather x1, blocking collectives, body(): lax.all_gather(center_weights, 'dev', axis=0, tiled=True)  30.7 us
    reduce_scatter x1, waiting for transfers between devices, body(): lax.psum_scatter(result, 'dev', scatter_dimension=0, tiled=True) * factor  20.1 us
    all_gather x1, waiting for transfers between devices, body(): predictions = jnp.sum(lax.all_gather(partial_pred, 'grp'), axis=0)  17.6 us
  transfers between devices with their start and end apart: 2, of which 2 were waited for; matrix products, arithmetic and copies ran while one was open for 1% of the time, Pallas kernels for 0%

profile of v1, /device:TPU:0, one launch (start us, length us, event | category | flops | bytes accessed | tf_op | source)
XLA Modules:
  0.0 171.3 jit_solution(2135346547136707944)
XLA Ops:
  7.2 0.0 copy-start
  7.2 0.0 copy-start.2
  7.2 0.0 all-gather.2.cloned.1.call-start
  7.2 32.9 %all_gather.9 = bf16[1024,128]{1,0:T(8,128)(2,1)S(1)} all-gather(bf16[128,128]{1,0:T(8,128)(2,1)} %param.13), channel_id=1, replica_groups=mesh['grp'=4,'dev'=8] {'dev'}, dimensions={0}, use_global_device_ids=true | all-gather | bytes 294912 | tf_op jit(solution)/shard_map/all_gather | solution.py:34
  40.1 0.2 multiply_reduce_fusion
  40.4 1.2 multiply_reduce_fusion.1
  41.5 0.8 copy.17
  42.4 30.7 %all_gather.10 = bf16[1024,64]{1,0:T(8,128)(2,1)S(1)} all-gather(bf16[128,64]{1,0:T(8,128)(2,1)S(1)} %copy.17), channel_id=1, replica_groups=mesh['grp'=4,'dev'=8] {'dev'}, dimensions={0}, use_global_device_ids=true | all-gather | bytes 147456 | tf_op jit(solution)/shard_map/all_gather | solution.py:35
  73.1 0.0 copy-done.2
  73.1 0.0 copy-start.4
  73.1 4.5 %while.32 = (s32[]{:T(128)}, f32[2,512,64]{1,0,2:T(2,128)S(1)}, f32[2,512]{1,0:T(2,128)S(1)}, f32[1024]{0:T(1024)S(1)}, bf16[2,512,128]{2,1,0:T(8,128)(2,1)S(1)}...) while((s32[]{:T(128)}, f32[2,512,64]{1,0,2:T(2,128)S(1)}, ...), condition=%wide.region_3.4_spmd, body=%wide.region_2.3_spmd.sunk | while | flops 203948032 | bytes 1321065 | solution.py:44
  73.1 0.9 fusion.81
  74.0 0.1 copy.29
  74.1 1.2 dynamic_update_slice.5
  75.4 0.9 fusion.81
  76.3 0.1 copy.29
  76.4 1.2 dynamic_update_slice.5
  77.6 0.0 copy-start.5
  77.6 0.9 all_gather_reshape.3
  78.6 0.0 all-gather.2.cloned.1.call-update
  78.6 0.0 reduce-scatter.2.cloned.1.call-start
  78.7 0.0 copy-done.4
  78.7 0.1 multiply_reduce_fusion.2
  78.8 17.6 %all-gather.2.cloned.1.call-done = f32[4,1024,64]{1,2,0:T(8,128)} async-done(((f32[1,1024,64]{1,2,0:T(8,128)}), f32[4,1024,64]{1,2,0:T(8,128)}) %all-gather.2.cloned.1.call-update) | async-done | bytes 1048592 | tf_op jit(solution)/shard_map/all_gather | solution.py:45
  96.4 1.3 reduce_sum.38
  97.7 0.0 copy-done.5
  97.7 0.0 copy-start.1
  97.8 0.2 copy.21
  98.0 0.5 copy-done.1
  98.5 1.7 while.33
  98.5 0.8 fusion.85
  99.3 0.8 fusion.85
  100.1 0.0 copy-start.3
  100.1 0.7 copy-done.3
  100.8 0.0 reduce-scatter.2.cloned.1.call-update
  100.8 0.0 copy-start.6
  100.9 1.2 while.34
  100.9 0.6 fusion.89
  101.5 0.6 fusion.89
  102.1 0.0 copy-done
  102.1 0.3 convolution_bitcast_fusion.1
  102.4 39.6 %psum.7 = f32[160,64]{0,1:T(8,128)S(1)} all-reduce(f32[160,64]{0,1:T(8,128)S(1)} %convolution_bitcast_fusion.1), channel_id=1, replica_groups=mesh['grp'=4,'dev'=8] {'grp','dev'}, use_global_device_ids=true, to_apply=%region_11.12 | all-reduce | flops 10240 | bytes 81920 | tf_op jit(solution)/shard_map/psum | solution.py:77
  142.0 0.0 copy-done.6
  142.0 0.9 convolution_bitcast_fusion
  142.9 20.1 %reduce-scatter.2.cloned.1.call-done = f32[128,64]{0,1:T(8,128)} async-done(((f32[1024,64]{0,1:T(8,128)}), f32[128,64]{0,1:T(8,128)}) %reduce-scatter.2.cloned.1.call-update) | async-done | bytes 32784 | tf_op jit(solution)/shard_map/reduce_scatter | solution.py:60
  163.1 1.4 broadcast_multiply_fusion
  (11 shorter events, 0.1 us)
Async XLA Ops:
  7.2 94.9 %copy-start = (bf16[512,160]{0,1:T(8,128)(2,1)S(1)}, bf16[512,160]{0,1:T(8,128)(2,1)}, u32[]{:S(2)}) copy-start(bf16[512,160]{0,1:T(8,128)(2,1)} %param.18) | copy-start | bytes 491524
  7.2 65.9 %copy-start.2 = (bf16[1024,128]{1,0:T(8,128)(2,1)S(1)}, bf16[1024,128]{1,0:T(8,128)(2,1)}, u32[]{:S(2)}) copy-start(bf16[1024,128]{1,0:T(8,128)(2,1)} %param.15) | copy-start | bytes 786436
  7.2 89.2 %all-gather.2.cloned.1.call-start = ((), (), s32[]{:S(2)}) async-start(), calls=%async_computation.1 | async-start | bytes 1310720 | tf_op jit(solution)/shard_map/all_gather | solution.py:45
  73.1 5.6 %copy-start.4 = (bf16[512,128]{1,0:T(8,128)(2,1)S(1)}, bf16[512,128]{1,0:T(8,128)(2,1)}, u32[]{:S(2)}) copy-start(bf16[512,128]{1,0:T(8,128)(2,1)} %param.17) | copy-start | bytes 393220
  77.6 20.1 %copy-start.5 = (bf16[1024,64]{0,1:T(8,128)(2,1)S(1)}, bf16[1024,64]{0,1:T(8,128)(2,1)}, u32[]{:S(2)}) copy-start(bf16[1024,64]{0,1:T(8,128)(2,1)} %param.16) | copy-start | bytes 393220
  78.6 84.5 %reduce-scatter.2.cloned.1.call-start = ((), (), s32[]{:S(2)}) async-start(), calls=%async_computation.2 | async-start | bytes 294912 | tf_op jit(solution)/shard_map/reduce_scatter | solution.py:60
  97.7 0.7 copy-start.1
  100.1 0.7 copy-start.3
  100.8 41.2 %copy-start.6 = (f32[160]{0:T(256)S(1)}, f32[160]{0:T(256)}, u32[]{:S(2)}) copy-start(f32[160]{0:T(256)} %param.19) | copy-start | bytes 1924
Sparse Core Ops, SparseCore 0:
  78.7 17.6 all-gather.1
  101.0 62.0 reduce-scatter.1
